TPU v7x, 128 devices: a whole 4x4x4 slice. The times are simulated.
128 devices in a mesh: seq: 32 (over z, y, core), tp: 4 (over x).
Axes of the slice: x: 4, y: 4, z: 4, core: 2. Of those that a mesh axis runs over, the one named last changes fastest.
Arguments:
- tokens: bfloat16 [32768, 2048], P('seq', 'tp'), may hold values from -8 to 8
- col_order: int32 [32768], P('seq'), may hold values from 0 to 32767, as said below
- in_gain: float32 [2, 2048], replicated, may hold values from 0.5 to 1.5
- w_in: bfloat16 [2, 2048, 2, 2048], P(None, None, None, 'tp'), may hold values from -0.125 to 0.125
- w_bc: bfloat16 [2, 2048, 256], replicated, may hold values from -0.0625 to 0.0625
- w_dt: bfloat16 [2, 2048, 32], P(None, None, 'tp'), may hold values from -2 to 2
- conv_x: float32 [2, 4, 2048], P(None, None, 'tp'), may hold values from -3 to 3
- conv_bc: float32 [2, 4, 256], replicated, may hold values from -3 to 3
- dt_bias: float32 [2, 32], P(None, 'tp'), may hold values from -1 to 0.5
- a_log: float32 [2, 32], P(None, 'tp'), may hold values from -16 to -2, as said below
- d_skip: float32 [2, 32], P(None, 'tp'), may hold values from 0.5 to 2
- out_gain: float32 [2, 2048], P(None, 'tp'), may hold values from 0.5 to 1.5
- w_out: bfloat16 [2, 2048, 2048], P(None, 'tp'), may hold values from -0.125 to 0.125
Outputs:
- mixed_out: bfloat16 [32768, 2048], P('seq', 'tp')
Inputs may be any that keep to these rules, and one draw needn't show every extreme that they name: `col_order`: A permutation of the 32768 positions of a frame of 64 rows and 512 columns stored row by row: the column order visits the columns one after another in a drawn order, each from top to bottom or from bottom to top as drawn. So every aligned block of 1024 positions takes exactly 32 row-order positions from each aligned block of 1024 row-order positions. Each head's decay rate exp(a_log) is either between about one in fifty and one in seventeen a step or between 0.3 / 32768 and 2 / 32768 a step.
All inputs are finite; a program needn't handle non-finite values.
Results may differ from a plain program's by a relative error of at most 0.024.
Values may be sent and summed in bfloat16 or wider, within the bound.
No kernel may reach another device: no remote copies, remote signals or barrier semaphores. Data moves between devices by JAX's collectives and lax.ppermute only.
A program may use at most 128 MiB of HBM per device.

v0:
```python
import jax
import jax.numpy as jnp
from jax import lax
from jax.sharding import Mesh
from jax.sharding import PartitionSpec as P

HEAD_DIM = 64
STATE = 128
STRETCH = 128
SEQ = ("seq_0", "seq_1", "seq_2")
highest = lax.Precision.HIGHEST
epsilon = 1e-05


def laid_out(blocks, dim):
    blocks = jnp.moveaxis(blocks, 0, dim)
    lengths = blocks.shape
    return blocks.reshape(*lengths[:dim], lengths[dim] * lengths[dim + 1], *lengths[dim + 2 :])


def sent_to_all(x, axis):
    devices = lax.axis_size(axis)
    return lax.all_to_all(jnp.broadcast_to(x[None], (devices, *x.shape)), axis, 0, 0, tiled=True)


def gathered_copies(x, axis, dim):
    return laid_out(sent_to_all(x, axis), dim)


def passed_along(x, axis, by):
    devices = lax.axis_size(axis)
    pairs = [(i, i + by) for i in range(devices) if 0 <= i + by < devices]
    return lax.ppermute(x, axis, pairs)


def in_blocks(x, dim, devices):
    lengths = x.shape
    blocks = x.reshape(*lengths[:dim], devices, lengths[dim] // devices, *lengths[dim + 1 :])
    return jnp.moveaxis(blocks, dim, 0)


def moved_by_axis(blocks, axes, turns):
    lengths = [lax.axis_size(a) for a in axes]
    blocks = blocks.reshape(*lengths, *blocks.shape[1:])
    for k in turns:
        blocks = lax.all_to_all(blocks, axes[k], split_axis=k, concat_axis=k, tiled=True)
    return blocks.reshape(-1, *blocks.shape[len(axes) :])


def exchange_by_chip(x, groups, turns, split_dim, concat_dim):
    devices = lax.axis_size(groups[0]) * lax.axis_size(groups[1])
    blocks = in_blocks(x, split_dim, devices)
    return laid_out(moved_by_axis(blocks, groups, turns), concat_dim)


def causal_mix(current, rim, taps):
    length = current.shape[0]
    extended = jnp.concatenate([rim, current], axis=0).astype(jnp.float32)
    mixed = jnp.zeros(current.shape, jnp.float32)
    for offset in range(taps.shape[0]):
        mixed = mixed + taps[offset] * extended[offset : offset + length]
    return mixed


def advance(state, pieces):
    factor, fresh = pieces
    return (factor[:, None, None] * state + fresh, state)


def incoming_state(local_end, device_log):
    count = lax.axis_size(SEQ)
    own_index = lax.axis_index(SEQ)
    gathered = gathered_copies(device_log, SEQ, 0).reshape(count, device_log.shape[0])
    before = jnp.cumsum(gathered, axis=0) - gathered
    earlier = (jnp.arange(count) < own_index)[:, None]
    own_prefix = jnp.sum(jnp.where(earlier, gathered, 0.0), axis=0)
    spans = jnp.where(earlier, own_prefix[None, :] - before - gathered, -jnp.inf)
    factors = jnp.exp(spans)
    return jnp.zeros(local_end.shape, jnp.float32) + jnp.einsum(
        "mh,mhpn->hpn",
        factors,
        lax.all_gather(local_end[None].astype(jnp.bfloat16), SEQ, axis=0, tiled=True).astype(
            jnp.float32
        ),
        precision=highest,
    )


def mixer(full, which, params):
    in_gain, w_in, w_bc, w_dt, conv_x, conv_bc, dt_bias, a_log, d_skip, out_gain, w_out = params
    row_count, model_width = full.shape
    inner = w_in.shape[3]
    head_count = inner // HEAD_DIM
    lag = conv_x.shape[1] - 1
    widen = full.astype(jnp.float32)
    scale = lax.rsqrt(jnp.mean(widen * widen, axis=-1, keepdims=True) + epsilon)
    normed = (widen * scale * in_gain[which]).astype(jnp.bfloat16)
    projected = jnp.dot(
        normed, w_in[which].reshape(model_width, 2 * inner), preferred_element_type=jnp.float32
    )
    pre_x = projected[:, :inner].astype(jnp.bfloat16)
    gate_z = projected[:, inner:].astype(jnp.bfloat16)
    pre_bc = jnp.dot(normed, w_bc[which], preferred_element_type=jnp.float32).astype(jnp.bfloat16)
    dt_raw = jnp.dot(normed, w_dt[which], preferred_element_type=jnp.float32)
    rim_x, rim_bc = passed_along((pre_x[row_count - lag :], pre_bc[row_count - lag :]), SEQ, 1)
    conv_out = jax.nn.silu(causal_mix(pre_x, rim_x, conv_x[which]))
    bc_out = jax.nn.silu(causal_mix(pre_bc, rim_bc, conv_bc[which]))
    step_size = jax.nn.softplus(dt_raw + dt_bias[which])
    decay_log = -step_size * jnp.exp(a_log[which])
    heads_in = conv_out.reshape(row_count, head_count, HEAD_DIM)
    feed = heads_in * step_size[:, :, None]
    blocks = row_count // STRETCH
    log_blocks = decay_log.reshape(blocks, STRETCH, head_count)
    b_blocks = bc_out[:, :STATE].reshape(blocks, STRETCH, STATE)
    c_blocks = bc_out[:, STATE:].reshape(blocks, STRETCH, STATE)
    feed_blocks = feed.reshape(blocks, STRETCH, head_count, HEAD_DIM)
    cumul = jnp.cumsum(log_blocks, axis=1)
    cumul_t = jnp.transpose(cumul, (0, 2, 1))
    lower = jnp.arange(STRETCH)[:, None] >= jnp.arange(STRETCH)[None, :]
    spread = jnp.where(lower[None, None], cumul_t[..., :, None] - cumul_t[..., None, :], -jnp.inf)
    intersection = jnp.einsum("cqn,ckn->cqk", c_blocks, b_blocks, precision=highest)
    inside = jnp.einsum(
        "chqk,ckhp->cqhp", intersection[:, None] * jnp.exp(spread), feed_blocks, precision=highest
    )
    to_end = jnp.exp(cumul_t[..., -1:] - cumul_t)
    fresh = jnp.einsum("chk,ckn,ckhp->chpn", to_end, b_blocks, feed_blocks, precision=highest)
    block_decay = jnp.exp(cumul_t[..., -1])
    start_state = jnp.zeros((head_count, HEAD_DIM, STATE), jnp.float32)
    local_end, entering = lax.scan(advance, start_state, (block_decay, fresh))
    carried = (
        jnp.einsum("cqn,chpn->cqhp", c_blocks, entering, precision=highest)
        * jnp.exp(cumul)[..., None]
    )
    block_sums = cumul[:, -1, :]
    prior = jnp.cumsum(block_sums, axis=0) - block_sums
    device_cumul = cumul + prior[:, None, :]
    device_log = jnp.sum(block_sums, axis=0)
    arriving = incoming_state(local_end, device_log)
    correction = (
        jnp.einsum("cqn,hpn->cqhp", c_blocks, arriving, precision=highest)
        * jnp.exp(device_cumul)[..., None]
    )
    ssd = (inside + carried + correction).reshape(row_count, head_count, HEAD_DIM) + d_skip[which][
        None, :, None
    ] * heads_in
    gated = ssd * jax.nn.silu(gate_z.astype(jnp.float32).reshape(row_count, head_count, HEAD_DIM))
    norm_scale = lax.rsqrt(jnp.mean(gated * gated, axis=-1, keepdims=True) + epsilon)
    mixed_heads = (
        (gated * norm_scale * out_gain[which].reshape(head_count, HEAD_DIM))
        .reshape(row_count, inner)
        .astype(jnp.bfloat16)
    )
    return jnp.dot(mixed_heads, w_out[which], preferred_element_type=jnp.float32)


def spread_features(piece):
    return lax.all_gather(piece, "tp", axis=1, tiled=True)


def collect_heads(partial_sum):
    return lax.psum_scatter(
        partial_sum.astype(jnp.bfloat16), "tp", scatter_dimension=1, tiled=True
    ).astype(jnp.float32)


def reorder_rows(stream, col_order):
    count = lax.axis_size(SEQ)
    row_count = stream.shape[0]
    block_rows = row_count // count
    source = col_order // row_count
    local_index = col_order % row_count
    grouping = jnp.argsort(source, stable=True)
    wanted = local_index[grouping].reshape(count, block_rows)
    asked = exchange_by_chip(wanted, (("seq_0", "seq_1"), "seq_2"), (1, 0), 0, 0)
    payload = stream[asked.reshape(-1)].reshape(count, block_rows, stream.shape[1])
    arrived = exchange_by_chip(payload, (("seq_0", "seq_1"), "seq_2"), (1, 0), 0, 0).reshape(
        row_count, stream.shape[1]
    )
    placement = jnp.argsort(grouping)
    return arrived[placement]


def body(
    tokens,
    col_order,
    in_gain,
    w_in,
    w_bc,
    w_dt,
    conv_x,
    conv_bc,
    dt_bias,
    a_log,
    d_skip,
    out_gain,
    w_out,
):
    params = (in_gain, w_in, w_bc, w_dt, conv_x, conv_bc, dt_bias, a_log, d_skip, out_gain, w_out)
    first_full = spread_features(tokens)
    first_part = mixer(first_full, 0, params)
    row_result = (tokens.astype(jnp.float32) + collect_heads(first_part)).astype(jnp.bfloat16)
    own_rows = reorder_rows(row_result, col_order)
    second_full = spread_features(own_rows)
    second_part = mixer(second_full, 1, params)
    return (own_rows.astype(jnp.float32) + collect_heads(second_part)).astype(jnp.bfloat16)


def solution(mesh):
    torus = Mesh(mesh.devices.reshape(4, 4, 2, mesh.shape["tp"]), ("seq_0", "seq_1", "seq_2", "tp"))
    return jax.shard_map(
        body,
        mesh=torus,
        in_specs=(
            P(SEQ, "tp"),
            P(SEQ),
            P(),
            P(None, None, None, "tp"),
            P(),
            P(None, None, "tp"),
            P(None, None, "tp"),
            P(),
            P(None, "tp"),
            P(None, "tp"),
            P(None, "tp"),
            P(None, "tp"),
            P(None, "tp", None),
        ),
        out_specs=P(SEQ, "tp"),
        check_vma=False,
    )
```

profile of v0, /device:TPU:1, one launch (start us, length us, event | category | flops | bytes accessed | tf_op | source)
XLA Modules:
  0.0 575.8 jit_solution(12658820675319592210)
XLA Ops:
  7.3 7.9 %fusion.98 = (bf16[1,2048,2,512]{3,2,1,0:T(2,128)(2,1)}, bf16[1,2048,2,512]{3,2,1,0:T(2,128)(2,1)S(1)}) fusion(bf16[2,2048,2,512]{3,2,1,0:T(2,128)(2,1)} %param.20), kind=kLoop, calls=%fused_computation.187 | loop fusion | bytes 16777216 | tf_op jit(solution)/shard_map/slice | solution.py:99
  20.9 39.6 %all-gather.8.cloned.1.call-done = bf16[1024,2048]{1,0:T(8,128)(2,1)} async-done(((bf16[1024,512]{1,0:T(8,128)(2,1)}), bf16[1024,2048]{1,0:T(8,128)(2,1)}) %all-gather.8.cloned.1.call-update) | async-done | bytes 4194320 | tf_op jit(solution)/shard_map/all_gather | solution.py:157
  63.9 7.2 %convolution_convert_fusion.3 = bf16[1024,1024]{1,0:T(8,128)(2,1)S(1)} fusion(bf16[2048,1024]{1,0:T(8,128)(2,1)} %bitcast.229, bf16[1024,2048]{1,0:T(8,128)(2,1)S(1)} %copy-done.14, f32[2048]{0:T(1024)S(1)} %bitcast.255, f32[1024]{0:T(1024)S(1)} %add_rsqrt_fusion.1), kind=kOutput, calls=%fused_computation.92 | convolution fusion | flops 4304404480 | bytes 10498048 | tf_op jit(solution)/shard_map/dot_general | solution.py:98
  75.0 23.3 %fusion.107 = f32[8,128,8]{2,0,1:T(8,128)S(1)} fusion(f32[8,128,8]{2,0,1:T(8,128)S(1)} %copy.146), kind=kOutput, calls=%fused_computation.197 | output fusion | flops 1040384 | bytes 65536 | tf_op jit(solution)/shard_map/jit(cumsum)/reduce_window_sum | solution.py:117
  129.5 19.8 %while.26 = (s32[]{:T(128)}, f32[8,64,128]{2,1,0:T(8,128)S(1)}, f32[8,8,64,128]{3,2,1,0:T(8,128)}, f32[8,8]{1,0:T(8,128)}, f32[8,8,64,128]{3,2,1,0:T(8,128)}, /*index=5*/s32[]{:T(128)}, s32[]{:T(128)}) while((s32[]{:T(128)}, f32[8,64,128]{2,1,0:T(8,128)S(1)}, f32[8,8,64,128]{3,2,1,0:T(8,128)}, f32[8,8]{1,0:T(8,128)}, ...), condition=%wide.region_3.4_spmd.clone, body=%wide.region_2.3_spmd.clone.sunk | while | flops 262147 | bytes 1311424 | solution.py:129
  153.1 7.8 %all-to-all-start = ((f32[32,1,8]{2,1,0:T(1,128)}), f32[32,1,8]{2,1,0:T(1,128)S(1)}, u32[]{:S(2)}, u32[]{:S(2)}) async-start(f32[32,1,8]{2,1,0:T(1,128)} %broadcast_in_dim.64), calls=%async_computation | async-start | bytes 32768 | tf_op jit(solution)/shard_map/all_to_all | solution.py:23
  176.1 9.7 %fusion.17 = f32[8,8,64,128]{3,2,1,0:T(8,128)} fusion(f32[8,128,8,64]{1,0,3,2:T(8,128)S(1)} %copy-done.18, f32[8,8,128]{2,1,0:T(8,128)S(1)} %copy.147, f32[8,128,128]{2,1,0:T(8,128)S(1)} %fusion.109, pred[128,128]{1,0:T(8,128)(4,1)S(1)} %iota_compare_fusion), kind=kOutput, calls=%fused_computation.30 | convolution fusion | flops 808452096 | bytes 4767744 | tf_op jit(solution)/shard_map/chqk,ckhp->cqhp/dot_general | solution.py:122
  185.7 11.7 %all-gather.10.cloned.1.call-done = bf16[256,64,128]{2,1,0:T(8,128)(2,1)} async-done(((bf16[8,64,128]{2,1,0:T(8,128)(2,1)}), bf16[256,64,128]{2,1,0:T(8,128)(2,1)}) %all-gather.10.cloned.1.call-update) | async-done | bytes 4194320 | tf_op jit(solution)/shard_map/all_gather | solution.py:82
  197.4 6.2 %fusion.10 = f32[8,1,64,128]{3,1,2,0:T(1,128)S(1)} fusion(f32[32,8,1,1]{0,2,3,1:T(1,128)S(1)} %copy.184, bf16[32,8,64,128]{3,2,1,0:T(8,128)(2,1)} %bitcast.226), kind=kOutput, calls=%fused_computation.23 | convolution fusion | flops 25165824 | bytes 4457472 | tf_op jit(solution)/shard_map/mh,mhpn->hpn/dot_general | solution.py:79
  218.6 8.5 %convolution_convert_fusion.1 = bf16[1024,2048]{1,0:T(8,128)(2,1)} fusion(bf16[2,512,2048]{2,1,0:T(8,128)(2,1)} %param.29, f32[1024,512]{1,0:T(8,128)} %copy.160, f32[1024,512]{1,0:T(8,128)} %reshape.289, f32[1024,512]{1,0:T(8,128)} %divide_multiply_fusion.1, f32[512]{0:T(512)S(1)} %bitcast.267, f32[512]{0:T(512)S(1)} %copy-done.39, ...), kind=kOutput, calls=%fused_computation.36 | convolution fusion | flops 2155347968 | bytes 13635584 | tf_op jit(solution)/shard_map/dot_general | solution.py:153
  242.5 11.0 %all_to_all.39 = s32[16,2,1,32]{3,2,1,0:T(1,128)S(1)} all-to-all(s32[16,2,1,32]{3,2,1,0:T(1,128)S(1)} %copy.162), channel_id=1, replica_groups=mesh['seq_0'=4,'seq_1'=4,'seq_2'=2,'tp'=4] {'seq_0','seq_1'}, dimensions={0} | all-to-all | bytes 8192 | tf_op jit(solution)/shard_map/all_to_all | solution.py:46
  254.8 18.2 %reduce-scatter.3.cloned.1.call-done = bf16[1024,512]{1,0:T(8,128)(2,1)} async-done(((bf16[1024,2048]{1,0:T(8,128)(2,1)}), bf16[1024,512]{1,0:T(8,128)(2,1)}) %reduce-scatter.3.cloned.1.call-update) | async-done | bytes 1048592 | tf_op jit(solution)/shard_map/reduce_scatter | solution.py:161
  284.5 6.7 %all-to-all-start.4 = ((bf16[16,2,1,32,512]{4,3,1,2,0:T(8,128)(2,1)}), bf16[16,2,1,32,512]{4,3,1,2,0:T(8,128)(2,1)S(1)}, u32[]{:S(2)}, u32[]{:S(2)}) async-start(bf16[16,2,1,32,512]{4,3,1,2,0:T(8,128)(2,1)} %copy.164), calls=%async_computation.5 | async-start | bytes 2097152 | tf_op jit(solution)/shard_map/all_to_all | solution.py:46
  295.6 11.9 %all-to-all-done.4 = bf16[16,2,1,32,512]{4,3,1,2,0:T(8,128)(2,1)S(1)} async-done(((bf16[16,2,1,32,512]{4,3,1,2,0:T(8,128)(2,1)}), bf16[16,2,1,32,512]{4,3,1,2,0:T(8,128)(2,1)S(1)}, u32[]{:S(2)}, u32[]{:S(2)}) %all-to-all-start.4) | async-done | bytes 1048608 | tf_op jit(solution)/shard_map/all_to_all | solution.py:46
  318.4 39.9 %all-gather.12.cloned.1.call-done = bf16[1024,2048]{1,0:T(8,128)(2,1)} async-done(((bf16[1024,512]{1,0:T(8,128)(2,1)}), bf16[1024,2048]{1,0:T(8,128)(2,1)}) %all-gather.12.cloned.1.call-update) | async-done | bytes 4194320 | tf_op jit(solution)/shard_map/all_gather | solution.py:157
  369.1 23.3 %fusion.108 = f32[8,128,8]{2,0,1:T(8,128)S(1)} fusion(f32[8,128,8]{2,0,1:T(8,128)S(1)} %copy.167), kind=kOutput, calls=%fused_computation.198 | output fusion | flops 1040384 | bytes 65536 | tf_op jit(solution)/shard_map/jit(cumsum)/reduce_window_sum | solution.py:117
  392.5 8.0 %convolution_convert_fusion.2 = bf16[1024,1024]{1,0:T(8,128)(2,1)S(1)} fusion(bf16[2048,1024]{1,0:T(8,128)(2,1)} %bitcast.230, bf16[1024,2048]{1,0:T(8,128)(2,1)} %all-gather.12.cloned.1.call-done, f32[2048]{0:T(1024)S(1)} %bitcast.254, f32[1024]{0:T(1024)S(1)} %add_rsqrt_fusion), kind=kOutput, calls=%fused_computation.91 | convolution fusion | flops 4304404480 | bytes 10498048 | tf_op jit(solution)/shard_map/dot_general | solution.py:98
  423.8 19.8 %while.27 = (s32[]{:T(128)}, f32[8,64,128]{2,1,0:T(8,128)S(1)}, f32[8,8,64,128]{3,2,1,0:T(8,128)}, f32[8,8]{1,0:T(8,128)}, f32[8,8,64,128]{3,2,1,0:T(8,128)}, /*index=5*/s32[]{:T(128)}, s32[]{:T(128)}) while((s32[]{:T(128)}, f32[8,64,128]{2,1,0:T(8,128)S(1)}, f32[8,8,64,128]{3,2,1,0:T(8,128)}, f32[8,8]{1,0:T(8,128)}, ...), condition=%wide.region_15.16_spmd.clone, body=%wide.region_14.15_spmd.clone.sunk | while | flops 262147 | bytes 1311424 | solution.py:129
  445.1 7.2 %all-to-all-start.5 = ((f32[32,1,8]{2,1,0:T(1,128)}), f32[32,1,8]{2,1,0:T(1,128)S(1)}, u32[]{:S(2)}, u32[]{:S(2)}) async-start(f32[32,1,8]{2,1,0:T(1,128)} %broadcast_in_dim.112), calls=%async_computation.6 | async-start | bytes 32768 | tf_op jit(solution)/shard_map/all_to_all | solution.py:23
  467.7 9.7 %fusion.12 = f32[8,8,64,128]{3,2,1,0:T(8,128)} fusion(f32[8,128,8,64]{1,0,3,2:T(8,128)S(1)} %copy-done.19, f32[8,8,128]{2,1,0:T(8,128)S(1)} %copy.168, f32[8,128,128]{2,1,0:T(8,128)S(1)} %fusion.111, pred[128,128]{1,0:T(8,128)(4,1)S(1)} %iota_compare_fusion), kind=kOutput, calls=%fused_computation.25 | convolution fusion | flops 808452096 | bytes 4767744 | tf_op jit(solution)/shard_map/chqk,ckhp->cqhp/dot_general | solution.py:122
  477.4 13.8 %all-gather.14.cloned.1.call-done = bf16[256,64,128]{2,1,0:T(8,128)(2,1)} async-done(((bf16[8,64,128]{2,1,0:T(8,128)(2,1)}), bf16[256,64,128]{2,1,0:T(8,128)(2,1)}) %all-gather.14.cloned.1.call-update) | async-done | bytes 4194320 | tf_op jit(solution)/shard_map/all_gather | solution.py:82
  491.1 6.0 %fusion.8 = f32[8,1,64,128]{3,1,2,0:T(1,128)S(1)} fusion(f32[32,8,1,1]{0,2,3,1:T(1,128)S(1)} %copy.189, bf16[32,8,64,128]{3,2,1,0:T(8,128)(2,1)} %bitcast.227), kind=kOutput, calls=%fused_computation.21 | convolution fusion | flops 25165824 | bytes 4457472 | tf_op jit(solution)/shard_map/mh,mhpn->hpn/dot_general | solution.py:79
  512.0 8.4 %convolution_convert_fusion = bf16[1024,2048]{1,0:T(8,128)(2,1)} fusion(bf16[2,512,2048]{2,1,0:T(8,128)(2,1)} %param.29, f32[1024,512]{1,0:T(8,128)} %copy.181, f32[1024,512]{1,0:T(8,128)} %reshape.290, f32[1024,512]{1,0:T(8,128)} %divide_multiply_fusion, f32[512]{0:T(512)S(1)} %bitcast.266, f32[512]{0:T(512)S(1)} %mul.565, bf16[1024,1024]{1,0:T(8,128)(2,1)} %copy-done.17), kind=kOutput, calls=%fused_computation.35 | convolution fusion | flops 2155347968 | bytes 13635584 | tf_op jit(solution)/shard_map/dot_general | solution.py:153
  520.5 45.8 %reduce-scatter.5.cloned.1.call-done = bf16[1024,512]{1,0:T(8,128)(2,1)} async-done(((bf16[1024,2048]{1,0:T(8,128)(2,1)}), bf16[1024,512]{1,0:T(8,128)(2,1)}) %reduce-scatter.5.cloned.1.call-update) | async-done | bytes 1048592 | tf_op jit(solution)/shard_map/reduce_scatter | solution.py:161
  (314 shorter events, 229.1 us)
Async XLA Ops:
  6.5 53.9 %all-gather.8.cloned.1.call-start = ((), (), s32[]{:S(2)}) async-start(), calls=%async_computation.8 | async-start | bytes 5242880 | tf_op jit(solution)/shard_map/all_gather | solution.py:157
  7.3 190.2 %all-gather.10.cloned.1.call-start = ((), (), s32[]{:S(2)}) async-start(), calls=%async_computation.11 | async-start | bytes 4325376 | tf_op jit(solution)/shard_map/all_gather | solution.py:82
  98.9 15.1 %collective-permute-start = (bf16[3,512]{1,0:T(4,128)(2,1)}, bf16[3,512]{1,0:T(4,128)(2,1)S(1)}, u32[]{:S(2)}, u32[]{:S(2)}) collective-permute-start(bf16[3,512]{1,0:T(4,128)(2,1)} %slice.314), channel_id=1, source_target_pairs={{0,4},{4,8},{8,12},{12,16},{16,20},{20,24},{24,28},{28,32},{32,36}... | collective-permute-start | bytes 9224 | tf_op jit(solution)/shard_map/ppermute | solution.py:33
  107.3 3.4 collective-permute-start.1
  129.5 20.5 %copy-start.47 = (f32[2,8]{1,0:T(2,128)S(1)}, f32[2,8]{1,0:T(2,128)}, u32[]{:S(2)}) copy-start(f32[2,8]{1,0:T(2,128)} %param.27) | copy-start | bytes 196
  129.5 22.3 %copy-start.37 = (f32[2,512]{1,0:T(2,128)S(1)}, f32[2,512]{1,0:T(2,128)}, u32[]{:S(2)}) copy-start(f32[2,512]{1,0:T(2,128)} %param.28) | copy-start | bytes 12292
  153.1 18.2 %all-to-all-start = ((f32[32,1,8]{2,1,0:T(1,128)}), f32[32,1,8]{2,1,0:T(1,128)S(1)}, u32[]{:S(2)}, u32[]{:S(2)}) async-start(f32[32,1,8]{2,1,0:T(1,128)} %broadcast_in_dim.64), calls=%async_computation | async-start | bytes 32768 | tf_op jit(solution)/shard_map/all_to_all | solution.py:23
  160.9 112.1 %reduce-scatter.3.cloned.1.call-start = ((), (), s32[]{:S(2)}) async-start(), calls=%async_computation.9 | async-start | bytes 5242880 | tf_op jit(solution)/shard_map/reduce_scatter | solution.py:161
  197.4 6.3 %copy-start.2 = (f32[64,8,8,128]{3,2,1,0:T(8,128)S(1)}, f32[64,8,8,128]{3,2,1,0:T(8,128)}, u32[]{:S(2)}) copy-start(f32[64,8,8,128]{3,2,1,0:T(8,128)} %copy-done.1) | copy-start | bytes 6291460
  197.4 6.3 %copy-start.21 = (f32[8,128,8,64]{1,3,2,0:T(8,128)S(1)}, f32[8,128,8,64]{1,3,2,0:T(8,128)}, u32[]{:S(2)}) copy-start(f32[8,128,8,64]{1,3,2,0:T(8,128)} %copy.159) | copy-start | bytes 6291460
  197.4 6.3 %copy-start.42 = (f32[8]{0:T(128)S(1)}, f32[8]{0:T(128)}, u32[]{:S(2)}) copy-start(f32[8]{0:T(128)} %copy-done.41) | copy-start | bytes 100
  232.2 40.8 %copy-start.11 = (bf16[1024,512]{1,0:T(8,128)(2,1)S(1)}, bf16[1024,512]{1,0:T(8,128)(2,1)}, u32[]{:S(2)}) copy-start(bf16[1024,512]{1,0:T(8,128)(2,1)} %param.17) | copy-start | bytes 3145732
  284.5 23.0 %all-to-all-start.4 = ((bf16[16,2,1,32,512]{4,3,1,2,0:T(8,128)(2,1)}), bf16[16,2,1,32,512]{4,3,1,2,0:T(8,128)(2,1)S(1)}, u32[]{:S(2)}, u32[]{:S(2)}) async-start(bf16[16,2,1,32,512]{4,3,1,2,0:T(8,128)(2,1)} %copy.164), calls=%async_computation.5 | async-start | bytes 2097152 | tf_op jit(solution)/shard_map/all_to_all | solution.py:46
  291.2 67.1 %all-gather.12.cloned.1.call-start = ((), (), s32[]{:S(2)}) async-start(), calls=%async_computation.12 | async-start | bytes 5242880 | tf_op jit(solution)/shard_map/all_gather | solution.py:157
  312.6 178.5 %all-gather.14.cloned.1.call-start = ((), (), s32[]{:S(2)}) async-start(), calls=%async_computation.13 | async-start | bytes 4325376 | tf_op jit(solution)/shard_map/all_gather | solution.py:82
  312.8 48.7 %copy-start.49 = (bf16[2,2048,256]{2,1,0:T(8,128)(2,1)S(1)}, bf16[2,2048,256]{2,1,0:T(8,128)(2,1)}, u32[]{:S(2)}) copy-start(bf16[2,2048,256]{2,1,0:T(8,128)(2,1)} %param.21) | copy-start | bytes 6291460
  318.4 43.2 %copy-start.29 = (f32[1,2048]{1,0:T(1,128)S(1)}, f32[1,2048]{1,0:T(1,128)}, u32[]{:S(2)}) copy-start(f32[1,2048]{1,0:T(1,128)} %get-tuple-element.155) | copy-start | bytes 24580
  363.7 41.9 %collective-permute-start.3 = (bf16[3,256]{1,0:T(4,128)(2,1)}, bf16[3,256]{1,0:T(4,128)(2,1)}, u32[]{:S(2)}, u32[]{:S(2)}) collective-permute-start(bf16[3,256]{1,0:T(4,128)(2,1)} %slice.336), channel_id=1, source_target_pairs={{0,4},{4,8},{8,12},{12,16},{16,20},{20,24},{24,28},{28,32},{32,36}... | collective-permute-start | bytes 4616 | tf_op jit(solution)/shard_map/ppermute | solution.py:33
  403.4 4.9 collective-permute-start.2
  423.8 20.5 %copy-start.40 = (f32[8]{0:T(128)S(1)}, f32[8]{0:T(128)}, u32[]{:S(2)}) copy-start(f32[8]{0:T(128)} %get-tuple-element.169) | copy-start | bytes 100
  445.1 17.9 %all-to-all-start.5 = ((f32[32,1,8]{2,1,0:T(1,128)}), f32[32,1,8]{2,1,0:T(1,128)S(1)}, u32[]{:S(2)}, u32[]{:S(2)}) async-start(f32[32,1,8]{2,1,0:T(1,128)} %broadcast_in_dim.112), calls=%async_computation.6 | async-start | bytes 32768 | tf_op jit(solution)/shard_map/all_to_all | solution.py:23
  452.3 114.0 %reduce-scatter.5.cloned.1.call-start = ((), (), s32[]{:S(2)}) async-start(), calls=%async_computation.10 | async-start | bytes 5242880 | tf_op jit(solution)/shard_map/reduce_scatter | solution.py:161
  491.1 6.0 %copy-start.20 = (f32[8,128,8,64]{1,3,2,0:T(8,128)S(1)}, f32[8,128,8,64]{1,3,2,0:T(8,128)}, u32[]{:S(2)}) copy-start(f32[8,128,8,64]{1,3,2,0:T(8,128)} %copy.180) | copy-start | bytes 6291460
  520.5 45.9 %copy-start = (bf16[1024,512]{1,0:T(8,128)(2,1)S(1)}, bf16[1024,512]{1,0:T(8,128)(2,1)}, u32[]{:S(2)}) copy-start(bf16[1024,512]{1,0:T(8,128)(2,1)} %gather_fusion.2) | copy-start | bytes 3145732
  (41 other events, 144.8 us)
Sparse Core Ops, SparseCore 0:
  9.0 51.3 all-gather.7
  150.1 47.2 all-gather.9
  227.2 45.7 reduce-scatter.2
  312.7 45.5 all-gather.11
  444.4 46.7 all-gather.13
  520.6 45.6 reduce-scatter.4
where the time goes:
time: 584 us; the launch traced here: 576 us
  waiting for transfers between devices  183 us (31%)
  other arithmetic  118 us (20%)
  local copies, waits for them, and re-layouts  110 us (19%)
  matrix products  97.5 us (17%)
  starting transfers between devices  33.7 us (6%)
  blocking collectives  19.4 us (3%)
  between operations  14.5 us (2%)
    all_gather x2, waiting for transfers between devices, spread_features(): return lax.all_gather(piece, 'tp', axis=1, tiled=True)  79.5 us
    reduce_scatter x2, waiting for transfers between devices, collect_heads(): lax.psum_scatter(partial_sum.astype(jnp.bfloat16), 'tp', scatter_dimensio...  64.1 us
    another operation x2, other arithmetic, mixer(): cumul = jnp.cumsum(log_blocks, axis=1)  46.6 us
    all_gather x2, waiting for transfers between devices, incoming_state(): lax.all_gather(local_end[None].astype(jnp.bfloat16), SEQ, axis=0, tiled=T...  25.5 us
    all_to_all x3, blocking collectives, moved_by_axis(): lax.all_to_all(blocks, axes[k], split_axis=k, concat_axis=k, tiled=True)  19.4 us
    dot_general x2, matrix products, mixer(): jnp.einsum('chqk,ckhp->cqhp', intersection[:, None] * jnp.exp(spread), fe...  19.3 us
    dot_general x2, matrix products, mixer(): jnp.dot(mixed_heads, w_out[which], preferred_element_type=jnp.float32)  17 us
    unnamed x111, local copies, waits for them, and re-layouts  16.7 us
  transfers between devices with their start and end apart: 13, of which 8 were waited for; matrix products, arithmetic and copies ran while one was open for 24% of the time, Pallas kernels for 0%

commit v1 on v0

--- a/solution.py
+++ b/solution.py
@@ -10,6 +10,19 @@
 SEQ = ("seq_0", "seq_1", "seq_2")
 highest = lax.Precision.HIGHEST
 epsilon = 1e-05
+
+
+def ring_gather(x, axis, dim):
+    ways = lax.axis_size(axis)
+    up = [(d, (d + 1) % ways) for d in range(ways)]
+    down = [(d, (d - 1) % ways) for d in range(ways)]
+    earlier, later = ([x], [x])
+    for _ in range(ways // 2):
+        earlier.append(lax.ppermute(earlier[-1], axis, up))
+    for _ in range((ways - 1) // 2):
+        later.append(lax.ppermute(later[-1], axis, down))
+    line = jnp.concatenate([*earlier[::-1], *later[1:]], axis=dim)
+    return jnp.roll(line, (lax.axis_index(axis) - ways // 2) * x.shape[dim], axis=dim)
 
 
 def laid_out(blocks, dim):
@@ -154,7 +167,7 @@
 
 
 def spread_features(piece):
-    return lax.all_gather(piece, "tp", axis=1, tiled=True)
+    return ring_gather(piece, "tp", 1)
 
 
 def collect_heads(partial_sum):

time: 584 us -> 592 us (1.014)
  waiting for transfers between devices: 183 us -> 166 us
  other arithmetic: 118 us -> 133 us
  starting transfers between devices: 33.7 us -> 45.1 us
    all_gather x2 -> x0, waiting for transfers between devices: 79.5 us -> none  [spread_features(): return lax.all_gather(piece, 'tp', axis=1, tiled=True)]
    ppermute x0 -> x6, waiting for transfers between devices: none -> 71.5 us  [the longest x4 71.5 us: ring_gather(): earlier.append(lax.ppermute(earlier[-1], axis, up))]
    reduce_sum x2, other arithmetic: 6.44 us -> 21.9 us  [mixer(): scale = lax.rsqrt(jnp.mean(widen * widen, axis=-1, keepdims=True) + epsilon)]
    all_gather x2, waiting for transfers between devices: 25.5 us -> 18.9 us  [incoming_state(): lax.all_gather(local_end[None].astype(jnp.bfloat16), SEQ, axis=0, tiled=T...]
    ppermute x0 -> x6, starting transfers between devices: none -> 6.53 us  [the longest x2 3.93 us: ring_gather(): later.append(lax.ppermute(later[-1], axis, down))]
    unnamed x111 -> x101, local copies, waits for them, and re-layouts: 16.7 us -> 16.4 us
  transfers between devices with their start and end apart: 13 -> 17, of which waited for: 8 -> 9; matrix products, arithmetic and copies ran while one was open for 24% -> 23% of each run, Pallas kernels for 0% -> 0%
where the time goes in v1:
time: 592 us; the launch traced here: 582 us
  waiting for transfers between devices  166 us (28%)
  other arithmetic  133 us (22%)
  local copies, waits for them, and re-layouts  106 us (18%)
  matrix products  98.2 us (17%)
  starting transfers between devices  45.1 us (8%)
  blocking collectives  19.4 us (3%)
  between operations  14.2 us (2%)
    ppermute x4, waiting for transfers between devices, ring_gather(): earlier.append(lax.ppermute(earlier[-1], axis, up))  71.5 us
    reduce_scatter x2, waiting for transfers between devices, collect_heads(): lax.psum_scatter(partial_sum.astype(jnp.bfloat16), 'tp', scatter_dimensio...  63.6 us
    another operation x2, other arithmetic, mixer(): cumul = jnp.cumsum(log_blocks, axis=1)  46.6 us
    reduce_sum x2, other arithmetic, mixer(): scale = lax.rsqrt(jnp.mean(widen * widen, axis=-1, keepdims=True) + epsilon)  21.9 us
    all_to_all x3, blocking collectives, moved_by_axis(): lax.all_to_all(blocks, axes[k], split_axis=k, concat_axis=k, tiled=True)  19.4 us
    dot_general x2, matrix products, mixer(): jnp.einsum('chqk,ckhp->cqhp', intersection[:, None] * jnp.exp(spread), fe...  19.3 us
    all_gather x2, waiting for transfers between devices, incoming_state(): lax.all_gather(local_end[None].astype(jnp.bfloat16), SEQ, axis=0, tiled=T...  18.9 us
    dot_general x2, matrix products, mixer(): jnp.dot(mixed_heads, w_out[which], preferred_element_type=jnp.float32)  16.9 us
  transfers between devices with their start and end apart: 17, of which 9 were waited for; matrix products, arithmetic and copies ran while one was open for 23% of the time, Pallas kernels for 0%

profile of v1, /device:TPU:1, one launch (start us, length us, event | category | flops | bytes accessed | tf_op | source)
XLA Modules:
  0.0 582.1 jit_solution(9972186400385697491)
XLA Ops:
  9.8 7.9 %fusion.114 = (bf16[1,2048,2,512]{3,2,1,0:T(2,128)(2,1)}, bf16[1,2048,2,512]{3,2,1,0:T(2,128)(2,1)S(1)}) fusion(bf16[2,2048,2,512]{3,2,1,0:T(2,128)(2,1)} %param.22), kind=kLoop, calls=%fused_computation.217 | loop fusion | bytes 16777216 | tf_op jit(solution)/shard_map/slice | solution.py:112
  21.6 10.9 %collective-permute-done = bf16[1024,512]{1,0:T(8,128)(2,1)S(1)} collective-permute-done((bf16[1024,512]{1,0:T(8,128)(2,1)}, bf16[1024,512]{1,0:T(8,128)(2,1)S(1)}, u32[]{:S(2)}, u32[]{:S(2)}) %collective-permute-start) | collective-permute-done | bytes 1048608 | tf_op jit(solution)/shard_map/ppermute | solution.py:21
  34.6 22.1 %collective-permute-done.1 = bf16[1024,512]{1,0:T(8,128)(2,1)S(1)} collective-permute-done((bf16[1024,512]{1,0:T(8,128)(2,1)S(1)}, bf16[1024,512]{1,0:T(8,128)(2,1)S(1)}, u32[]{:S(2)}, u32[]{:S(2)}) %collective-permute-start.1) | collective-permute-done | bytes 1048608 | tf_op jit(solution)/shard_map/ppermute | solution.py:21
  56.7 11.5 %fusion.2 = (f32[1024]{0:T(1024)S(1)}, bf16[1024,2048]{1,0:T(8,128)(2,1)S(1)}) fusion(s32[]{:T(128)S(6)} %select_n.80, bf16[1024,512]{1,0:T(8,128)(2,1)S(1)} %collective-permute-done.2, bf16[1024,512]{1,0:T(8,128)(2,1)S(1)} %copy-done.12, bf16[1024,512]{1,0:T(8,128)(2,1)S(1)} %collective-permute-done, bf16[1024,512]{1,0:T(8,128)(2,1)S(1)} %collective-permute-done.1), kind=kLoop, calls=%fused_computation.15 | loop fusion | flops 39844864 | bytes 8392708 | tf_op jit(solution)/shard_map/reduce_sum | solution.py:109
  77.0 23.3 %fusion.123 = f32[8,128,8]{2,0,1:T(8,128)S(1)} fusion(f32[8,128,8]{2,0,1:T(8,128)S(1)} %copy.146), kind=kOutput, calls=%fused_computation.227 | output fusion | flops 1040384 | bytes 65536 | tf_op jit(solution)/shard_map/jit(cumsum)/reduce_window_sum | solution.py:130
  132.7 19.7 %while.26 = (s32[]{:T(128)}, f32[8,64,128]{2,1,0:T(8,128)S(1)}, f32[8,8,64,128]{3,2,1,0:T(8,128)}, f32[8,8]{1,0:T(8,128)}, f32[8,8,64,128]{3,2,1,0:T(8,128)}, /*index=5*/s32[]{:T(128)}, s32[]{:T(128)}) while((s32[]{:T(128)}, f32[8,64,128]{2,1,0:T(8,128)S(1)}, f32[8,8,64,128]{3,2,1,0:T(8,128)}, f32[8,8]{1,0:T(8,128)}, ...), condition=%wide.region_3.5_spmd.clone, body=%wide.region_2.4_spmd.clone.sunk | while | flops 262147 | bytes 1311424 | solution.py:142
  156.3 8.3 %all-to-all-start = ((f32[32,1,8]{2,1,0:T(1,128)}), f32[32,1,8]{2,1,0:T(1,128)S(1)}, u32[]{:S(2)}, u32[]{:S(2)}) async-start(f32[32,1,8]{2,1,0:T(1,128)} %broadcast_in_dim.64), calls=%async_computation | async-start | bytes 32768 | tf_op jit(solution)/shard_map/all_to_all | solution.py:36
  179.8 9.6 %fusion.31 = f32[8,8,64,128]{3,2,1,0:T(8,128)} fusion(f32[8,128,8,64]{1,0,3,2:T(8,128)S(1)} %copy-done.16, f32[8,8,128]{2,1,0:T(8,128)S(1)} %copy.147, f32[8,128,128]{2,1,0:T(8,128)S(1)} %fusion.125, pred[128,128]{1,0:T(8,128)(4,1)S(1)} %iota_compare_fusion), kind=kOutput, calls=%fused_computation.60 | convolution fusion | flops 808452096 | bytes 4767744 | tf_op jit(solution)/shard_map/chqk,ckhp->cqhp/dot_general | solution.py:135
  189.4 10.2 %all-gather.5.cloned.1.call-done = bf16[256,64,128]{2,1,0:T(8,128)(2,1)} async-done(((bf16[8,64,128]{2,1,0:T(8,128)(2,1)}), bf16[256,64,128]{2,1,0:T(8,128)(2,1)}) %all-gather.5.cloned.1.call-update) | async-done | bytes 4194320 | tf_op jit(solution)/shard_map/all_gather | solution.py:95
  220.8 8.5 %convolution_convert_fusion.1 = bf16[1024,2048]{1,0:T(8,128)(2,1)} fusion(bf16[2,512,2048]{2,1,0:T(8,128)(2,1)} %param.31, f32[1024,512]{1,0:T(8,128)} %copy.160, f32[1024,512]{1,0:T(8,128)} %reshape.288, f32[1024,512]{1,0:T(8,128)} %divide_multiply_fusion.1, f32[512]{0:T(512)S(1)} %bitcast.267, f32[512]{0:T(512)S(1)} %copy-done.34, ...), kind=kOutput, calls=%fused_computation.66 | convolution fusion | flops 2155347968 | bytes 13635584 | tf_op jit(solution)/shard_map/dot_general | solution.py:166
  244.7 10.9 %all_to_all.39 = s32[16,2,1,32]{3,2,1,0:T(1,128)S(1)} all-to-all(s32[16,2,1,32]{3,2,1,0:T(1,128)S(1)} %copy.162), channel_id=1, replica_groups=mesh['seq_0'=4,'seq_1'=4,'seq_2'=2,'tp'=4] {'seq_0','seq_1'}, dimensions={0} | all-to-all | bytes 8192 | tf_op jit(solution)/shard_map/all_to_all | solution.py:59
  256.9 18.0 %reduce-scatter.3.cloned.1.call-done = bf16[1024,512]{1,0:T(8,128)(2,1)} async-done(((bf16[1024,2048]{1,0:T(8,128)(2,1)}), bf16[1024,512]{1,0:T(8,128)(2,1)}) %reduce-scatter.3.cloned.1.call-update) | async-done | bytes 1048592 | tf_op jit(solution)/shard_map/reduce_scatter | solution.py:174
  297.5 11.9 %all-to-all-done.4 = bf16[16,2,1,32,512]{4,3,1,2,0:T(8,128)(2,1)S(1)} async-done(((bf16[16,2,1,32,512]{4,3,1,2,0:T(8,128)(2,1)}), bf16[16,2,1,32,512]{4,3,1,2,0:T(8,128)(2,1)S(1)}, u32[]{:S(2)}, u32[]{:S(2)}) %all-to-all-start.4) | async-done | bytes 1048608 | tf_op jit(solution)/shard_map/all_to_all | solution.py:59
  316.1 21.1 %collective-permute-done.5 = bf16[1024,512]{1,0:T(8,128)(2,1)S(1)} collective-permute-done((bf16[1024,512]{1,0:T(8,128)(2,1)S(1)}, bf16[1024,512]{1,0:T(8,128)(2,1)S(1)}, u32[]{:S(2)}, u32[]{:S(2)}) %collective-permute-start.5) | collective-permute-done | bytes 1048608 | tf_op jit(solution)/shard_map/ppermute | solution.py:21
  342.8 17.5 %collective-permute-done.6 = bf16[1024,512]{1,0:T(8,128)(2,1)} collective-permute-done((bf16[1024,512]{1,0:T(8,128)(2,1)S(1)}, bf16[1024,512]{1,0:T(8,128)(2,1)}, u32[]{:S(2)}, u32[]{:S(2)}) %collective-permute-start.6) | collective-permute-done | bytes 1048608 | tf_op jit(solution)/shard_map/ppermute | solution.py:21
  360.3 10.4 %fusion.5 = (f32[1024]{0:T(1024)S(1)}, bf16[1024,2048]{1,0:T(8,128)(2,1)S(1)}) fusion(s32[]{:T(128)S(6)} %select_n.80, bf16[1024,512]{1,0:T(8,128)(2,1)} %collective-permute-done.7, bf16[1024,512]{1,0:T(8,128)(2,1)S(1)} %gather_fusion.2, bf16[1024,512]{1,0:T(8,128)(2,1)S(1)} %collective-permute-done.5, bf16[1024,512]{1,0:T(8,128)(2,1)} %collective-permute-done.6), kind=kLoop, calls=%fused_computation.18 | loop fusion | flops 39844864 | bytes 8392708 | tf_op jit(solution)/shard_map/reduce_sum | solution.py:109
  380.1 23.3 %fusion.124 = f32[8,128,8]{2,0,1:T(8,128)S(1)} fusion(f32[8,128,8]{2,0,1:T(8,128)S(1)} %copy.167), kind=kOutput, calls=%fused_computation.228 | output fusion | flops 1040384 | bytes 65536 | tf_op jit(solution)/shard_map/jit(cumsum)/reduce_window_sum | solution.py:130
  403.5 8.0 %convolution_convert_fusion.2 = bf16[1024,1024]{1,0:T(8,128)(2,1)S(1)} fusion(bf16[2048,1024]{1,0:T(8,128)(2,1)} %bitcast.230, bf16[1024,2048]{1,0:T(8,128)(2,1)} %copy-done.10, f32[2048]{0:T(1024)S(1)} %bitcast.254, f32[1024]{0:T(1024)S(1)} %add_rsqrt_fusion), kind=kOutput, calls=%fused_computation.121 | convolution fusion | flops 4304404480 | bytes 10498048 | tf_op jit(solution)/shard_map/dot_general | solution.py:111
  433.2 14.3 %while.27 = (s32[]{:T(128)}, f32[8,64,128]{2,1,0:T(8,128)S(1)}, f32[8,8,64,128]{3,2,1,0:T(8,128)}, f32[8,8]{1,0:T(8,128)S(1)}, f32[8,8,64,128]{3,2,1,0:T(8,128)}, /*index=5*/s32[]{:T(128)}, s32[]{:T(128)}) while((s32[]{:T(128)}, f32[8,64,128]{2,1,0:T(8,128)S(1)}, f32[8,8,64,128]{3,2,1,0:T(8,128)}, f32[8,8]{1,0:T(8,128)S(1)}, ...), condition=%wide.region_15.17_spmd.clone, body=%wide.region_14.16_spmd.clone.sunk | while | flops 262147 | bytes 1311424 | solution.py:142
  449.0 6.8 %all-to-all-start.5 = ((f32[32,1,8]{2,1,0:T(1,128)}), f32[32,1,8]{2,1,0:T(1,128)S(1)}, u32[]{:S(2)}, u32[]{:S(2)}) async-start(f32[32,1,8]{2,1,0:T(1,128)} %broadcast_in_dim.112), calls=%async_computation.6 | async-start | bytes 32768 | tf_op jit(solution)/shard_map/all_to_all | solution.py:36
  474.8 9.7 %fusion.26 = f32[8,8,64,128]{3,2,1,0:T(8,128)} fusion(f32[8,128,8,64]{1,0,3,2:T(8,128)S(1)} %copy-done.17, f32[8,8,128]{2,1,0:T(8,128)S(1)} %copy.168, f32[8,128,128]{2,1,0:T(8,128)S(1)} %fusion.127, pred[128,128]{1,0:T(8,128)(4,1)S(1)} %iota_compare_fusion), kind=kOutput, calls=%fused_computation.55 | convolution fusion | flops 808452096 | bytes 4767744 | tf_op jit(solution)/shard_map/chqk,ckhp->cqhp/dot_general | solution.py:135
  484.5 8.7 %all-gather.7.cloned.1.call-done = bf16[256,64,128]{2,1,0:T(8,128)(2,1)} async-done(((bf16[8,64,128]{2,1,0:T(8,128)(2,1)}), bf16[256,64,128]{2,1,0:T(8,128)(2,1)}) %all-gather.7.cloned.1.call-update) | async-done | bytes 4194320 | tf_op jit(solution)/shard_map/all_gather | solution.py:95
  518.8 8.4 %convolution_convert_fusion = bf16[1024,2048]{1,0:T(8,128)(2,1)} fusion(bf16[2,512,2048]{2,1,0:T(8,128)(2,1)} %param.31, f32[1024,512]{1,0:T(8,128)} %copy.181, f32[1024,512]{1,0:T(8,128)} %reshape.289, f32[1024,512]{1,0:T(8,128)} %divide_multiply_fusion, f32[512]{0:T(512)S(1)} %bitcast.266, f32[512]{0:T(512)S(1)} %mul.570, bf16[1024,1024]{1,0:T(8,128)(2,1)} %copy-done.15), kind=kOutput, calls=%fused_computation.65 | convolution fusion | flops 2155347968 | bytes 13635584 | tf_op jit(solution)/shard_map/dot_general | solution.py:166
  527.3 45.6 %reduce-scatter.5.cloned.1.call-done = bf16[1024,512]{1,0:T(8,128)(2,1)} async-done(((bf16[1024,2048]{1,0:T(8,128)(2,1)}), bf16[1024,512]{1,0:T(8,128)(2,1)}) %reduce-scatter.5.cloned.1.call-update) | async-done | bytes 1048592 | tf_op jit(solution)/shard_map/reduce_scatter | solution.py:174
  (310 shorter events, 254.9 us)
Async XLA Ops:
  6.5 193.1 %all-gather.5.cloned.1.call-start = ((), (), s32[]{:S(2)}) async-start(), calls=%async_computation.10 | async-start | bytes 4325376 | tf_op jit(solution)/shard_map/all_gather | solution.py:95
  6.5 26.0 %collective-permute-start = (bf16[1024,512]{1,0:T(8,128)(2,1)}, bf16[1024,512]{1,0:T(8,128)(2,1)S(1)}, u32[]{:S(2)}, u32[]{:S(2)}) collective-permute-start(bf16[1024,512]{1,0:T(8,128)(2,1)} %param.19), channel_id=1, source_target_pairs={{0,1},{1,2},{2,3},{3,0},{4,5},{5,6},{6,7},{7,4},{8,9},{9,10},{10,1... | collective-permute-start | bytes 3145736 | tf_op jit(solution)/shard_map/ppermute | solution.py:21
  8.6 26.0 %collective-permute-start.2 = (bf16[1024,512]{1,0:T(8,128)(2,1)}, bf16[1024,512]{1,0:T(8,128)(2,1)S(1)}, u32[]{:S(2)}, u32[]{:S(2)}) collective-permute-start(bf16[1024,512]{1,0:T(8,128)(2,1)} %param.19), channel_id=1, source_target_pairs={{0,3},{1,0},{2,1},{3,2},{4,7},{5,4},{6,5},{7,6},{8,11},{9,8},{10,9... | collective-permute-start | bytes 3145736 | tf_op jit(solution)/shard_map/ppermute | solution.py:23
  17.8 38.9 %copy-start.12 = (bf16[1024,512]{1,0:T(8,128)(2,1)S(1)}, bf16[1024,512]{1,0:T(8,128)(2,1)}, u32[]{:S(2)}) copy-start(bf16[1024,512]{1,0:T(8,128)(2,1)} %param.19) | copy-start | bytes 3145732
  32.5 24.2 %collective-permute-start.1 = (bf16[1024,512]{1,0:T(8,128)(2,1)S(1)}, bf16[1024,512]{1,0:T(8,128)(2,1)S(1)}, u32[]{:S(2)}, u32[]{:S(2)}) collective-permute-start(bf16[1024,512]{1,0:T(8,128)(2,1)S(1)} %collective-permute-done), channel_id=1, source_target_pairs={{0,1},{1,2},{2,3},{3,0},{4,5},{5,6},{6,7},{7,4},{8,9},{9,10},{10,1... | collective-permute-start | bytes 3145736 | tf_op jit(solution)/shard_map/ppermute | solution.py:21
  34.6 33.6 %copy-start.9 = (bf16[256,8,2,512]{3,1,2,0:T(8,128)(2,1)S(1)}, bf16[256,8,2,512]{3,1,2,0:T(8,128)(2,1)}, u32[]{:S(2)}) copy-start(bf16[256,8,2,512]{3,1,2,0:T(8,128)(2,1)} %copy.200) | copy-start | bytes 12582916
  105.3 8.4 %collective-permute-start.4 = (bf16[3,256]{1,0:T(4,128)(2,1)}, bf16[3,256]{1,0:T(4,128)(2,1)}, u32[]{:S(2)}, u32[]{:S(2)}) collective-permute-start(bf16[3,256]{1,0:T(4,128)(2,1)} %slice.320), channel_id=1, source_target_pairs={{0,4},{4,8},{8,12},{12,16},{16,20},{20,24},{24,28},{28,32},{32,36}... | collective-permute-start | bytes 4616 | tf_op jit(solution)/shard_map/ppermute | solution.py:46
  111.4 5.8 %collective-permute-start.3 = (bf16[3,512]{1,0:T(4,128)(2,1)}, bf16[3,512]{1,0:T(4,128)(2,1)S(1)}, u32[]{:S(2)}, u32[]{:S(2)}) collective-permute-start(bf16[3,512]{1,0:T(4,128)(2,1)} %slice.314), channel_id=1, source_target_pairs={{0,4},{4,8},{8,12},{12,16},{16,20},{20,24},{24,28},{28,32},{32,36}... | collective-permute-start | bytes 9224 | tf_op jit(solution)/shard_map/ppermute | solution.py:46
  132.7 20.5 %copy-start.42 = (f32[2,8]{1,0:T(2,128)S(1)}, f32[2,8]{1,0:T(2,128)}, u32[]{:S(2)}) copy-start(f32[2,8]{1,0:T(2,128)} %param.29) | copy-start | bytes 196
  132.7 22.3 %copy-start.32 = (f32[2,512]{1,0:T(2,128)S(1)}, f32[2,512]{1,0:T(2,128)}, u32[]{:S(2)}) copy-start(f32[2,512]{1,0:T(2,128)} %param.30) | copy-start | bytes 12292
  156.3 18.7 %all-to-all-start = ((f32[32,1,8]{2,1,0:T(1,128)}), f32[32,1,8]{2,1,0:T(1,128)S(1)}, u32[]{:S(2)}, u32[]{:S(2)}) async-start(f32[32,1,8]{2,1,0:T(1,128)} %broadcast_in_dim.64), calls=%async_computation | async-start | bytes 32768 | tf_op jit(solution)/shard_map/all_to_all | solution.py:36
  164.6 110.3 %reduce-scatter.3.cloned.1.call-start = ((), (), s32[]{:S(2)}) async-start(), calls=%async_computation.8 | async-start | bytes 5242880 | tf_op jit(solution)/shard_map/reduce_scatter | solution.py:174
  234.4 40.6 %copy-start.13 = (bf16[1024,512]{1,0:T(8,128)(2,1)S(1)}, bf16[1024,512]{1,0:T(8,128)(2,1)}, u32[]{:S(2)}) copy-start(bf16[1024,512]{1,0:T(8,128)(2,1)} %param.19) | copy-start | bytes 3145732
  286.4 23.0 %all-to-all-start.4 = ((bf16[16,2,1,32,512]{4,3,1,2,0:T(8,128)(2,1)}), bf16[16,2,1,32,512]{4,3,1,2,0:T(8,128)(2,1)S(1)}, u32[]{:S(2)}, u32[]{:S(2)}) async-start(bf16[16,2,1,32,512]{4,3,1,2,0:T(8,128)(2,1)} %copy.164), calls=%async_computation.5 | async-start | bytes 2097152 | tf_op jit(solution)/shard_map/all_to_all | solution.py:59
  293.1 200.1 %all-gather.7.cloned.1.call-start = ((), (), s32[]{:S(2)}) async-start(), calls=%async_computation.11 | async-start | bytes 4325376 | tf_op jit(solution)/shard_map/all_gather | solution.py:95
  313.4 23.8 %collective-permute-start.5 = (bf16[1024,512]{1,0:T(8,128)(2,1)S(1)}, bf16[1024,512]{1,0:T(8,128)(2,1)S(1)}, u32[]{:S(2)}, u32[]{:S(2)}) collective-permute-start(bf16[1024,512]{1,0:T(8,128)(2,1)S(1)} %gather_fusion.2), channel_id=1, source_target_pairs={{0,1},{1,2},{2,3},{3,0},{4,5},{5,6},{6,7},{7,4},{8,9},{9,10},{10,1... | collective-permute-start | bytes 3145736 | tf_op jit(solution)/shard_map/ppermute | solution.py:21
  313.5 29.3 %collective-permute-start.7 = (bf16[1024,512]{1,0:T(8,128)(2,1)S(1)}, bf16[1024,512]{1,0:T(8,128)(2,1)}, u32[]{:S(2)}, u32[]{:S(2)}) collective-permute-start(bf16[1024,512]{1,0:T(8,128)(2,1)S(1)} %gather_fusion.2), channel_id=1, source_target_pairs={{0,3},{1,0},{2,1},{3,2},{4,7},{5,4},{6,5},{7,6},{8,11},{9,8},{10,9... | collective-permute-start | bytes 3145736 | tf_op jit(solution)/shard_map/ppermute | solution.py:23
  337.2 23.1 %collective-permute-start.6 = (bf16[1024,512]{1,0:T(8,128)(2,1)S(1)}, bf16[1024,512]{1,0:T(8,128)(2,1)}, u32[]{:S(2)}, u32[]{:S(2)}) collective-permute-start(bf16[1024,512]{1,0:T(8,128)(2,1)S(1)} %collective-permute-done.5), channel_id=1, source_target_pairs={{0,1},{1,2},{2,3},{3,0},{4,5},{5,6},{6,7},{7,4},{8,9},{9,10},{10,1... | collective-permute-start | bytes 3145736 | tf_op jit(solution)/shard_map/ppermute | solution.py:21
  342.8 27.9 %copy-start.26 = (f32[1,2048]{1,0:T(1,128)S(1)}, f32[1,2048]{1,0:T(1,128)}, u32[]{:S(2)}) copy-start(f32[1,2048]{1,0:T(1,128)} %get-tuple-element.160) | copy-start | bytes 24580
  342.8 27.9 %copy-start.44 = (bf16[2,2048,256]{2,1,0:T(8,128)(2,1)S(1)}, bf16[2,2048,256]{2,1,0:T(8,128)(2,1)}, u32[]{:S(2)}) copy-start(bf16[2,2048,256]{2,1,0:T(8,128)(2,1)} %param.23) | copy-start | bytes 6291460
  372.1 44.2 %collective-permute-start.9 = (bf16[3,256]{1,0:T(4,128)(2,1)S(1)}, bf16[3,256]{1,0:T(4,128)(2,1)S(1)}, u32[]{:S(2)}, u32[]{:S(2)}) collective-permute-start(bf16[3,256]{1,0:T(4,128)(2,1)S(1)} %slice.336), channel_id=1, source_target_pairs={{0,4},{4,8},{8,12},{12,16},{16,20},{20,24},{24,28},{28,32},{32,36}... | collective-permute-start | bytes 4616 | tf_op jit(solution)/shard_map/ppermute | solution.py:46
  414.1 3.1 collective-permute-start.8
  449.0 19.3 %all-to-all-start.5 = ((f32[32,1,8]{2,1,0:T(1,128)}), f32[32,1,8]{2,1,0:T(1,128)S(1)}, u32[]{:S(2)}, u32[]{:S(2)}) async-start(f32[32,1,8]{2,1,0:T(1,128)} %broadcast_in_dim.112), calls=%async_computation.6 | async-start | bytes 32768 | tf_op jit(solution)/shard_map/all_to_all | solution.py:36
  455.8 117.0 %reduce-scatter.5.cloned.1.call-start = ((), (), s32[]{:S(2)}) async-start(), calls=%async_computation.9 | async-start | bytes 5242880 | tf_op jit(solution)/shard_map/reduce_scatter | solution.py:174
  (40 other events, 213.0 us)
Sparse Core Ops, SparseCore 0:
  153.2 46.3 all-gather.4
  229.4 45.4 reduce-scatter.2
  448.3 44.7 all-gather.6
  527.4 45.4 reduce-scatter.4
